TPU v7x, 32 devices: a whole 2x2x4 slice. The times are simulated.
32 devices in a mesh: groups: 2 (over x), width: 16 (over z, y, core).
Axes of the slice: x: 2, y: 2, z: 4, core: 2. Of those that a mesh axis runs over, the one named last changes fastest.
Arguments:
- stream_in: bfloat16 [2, 128, 8192], P(None, 'groups', 'width'), parts along dimension 1, may hold values from -16 to 16
- norm_gain: float32 [2, 8192], replicated, may hold values from 0.1 to 1.9
- w_gate: bfloat16 [2, 8192, 14336], P(None, None, 'width'), may hold values from -0.0625 to 0.0625
- w_up: bfloat16 [2, 8192, 14336], P(None, None, 'width'), may hold values from -0.0625 to 0.0625
- w_down: bfloat16 [2, 14336, 8192], P(None, 'width'), may hold values from -0.0625 to 0.0625
Outputs:
- stream_out: bfloat16 [2, 128, 8192], P(None, 'groups', 'width'), parts along dimension 1
There are 2 independent parts, one for each index of `groups`. A program takes and returns all parts, laid end to end along the dimension named above; an argument that names none is the same for every part. Nothing has to cross between parts.
All inputs are finite; a program needn't handle non-finite values.
Results may differ from a plain program's by a relative error of at most 0.012.
Values may be sent and summed in bfloat16 or wider, within the bound.
A program may use at most 192 MiB of HBM per device.

v0:
```python
import jax
import jax.numpy as jnp
from jax import lax
from jax.sharding import PartitionSpec as P

LAYERS = 2
MICRO = 2


def body(stream_in, norm_gain, w_gate, w_up, w_down):
    width_local = stream_in.shape[2]
    offset = lax.axis_index("width") * width_local
    starts = [
        lax.all_gather(stream_in[micro_index], "width", axis=1, tiled=True)
        for micro_index in range(MICRO)
    ]
    results = []
    for micro_index in range(MICRO):
        stream = starts[micro_index]
        for depth in range(LAYERS):
            stream_f = stream.astype(jnp.float32)
            meansq = jnp.mean(stream_f * stream_f, axis=1, keepdims=True)
            normed = (stream_f * lax.rsqrt(meansq + 1e-05) * norm_gain[depth]).astype(jnp.bfloat16)
            gate_out = jnp.dot(normed, w_gate[depth], preferred_element_type=jnp.float32)
            up_out = jnp.dot(normed, w_up[depth], preferred_element_type=jnp.float32)
            hidden = (jax.nn.silu(gate_out) * up_out).astype(jnp.bfloat16)
            partials = jnp.dot(hidden, w_down[depth], preferred_element_type=jnp.float32)
            branch = lax.psum(partials, "width")
            stream = (stream_f + branch).astype(jnp.bfloat16)
        results.append(stream)
    results = [lax.dynamic_slice_in_dim(stream, offset, width_local, 1) for stream in results]
    return jnp.stack(results)


def solution(mesh):
    return jax.shard_map(
        body,
        mesh=mesh,
        in_specs=(
            P(None, "groups", "width"),
            P(),
            P(None, None, "width"),
            P(None, None, "width"),
            P(None, "width", None),
        ),
        out_specs=P(None, "groups", "width"),
        check_vma=False,
    )
```

profile of v0, /device:TPU:0, one launch (start us, length us, event | category | flops | bytes accessed | tf_op | source)
XLA Modules:
  0.0 415.5 jit_solution(16510495588360910265)
XLA Ops:
  6.5 0.0 all-gather.5.cloned.1.call-start
  6.5 1.5 fusion.118
  8.1 0.0 all-gather.5.cloned.1.call-update
  8.1 0.0 all-gather.7.cloned.1.call-start
  8.1 0.7 all-gather.7.cloned.1.call-update
  8.8 0.0 all-reduce.7.cloned.1.call-start
  8.9 1.0 fusion.119
  9.9 39.0 %all-gather.5.cloned.1.call-done = bf16[1,64,8192]{2,1,0:T(8,128)(2,1)} async-done(((bf16[1,64,512]{2,1,0:T(8,128)(2,1)}), bf16[1,64,8192]{2,1,0:T(8,128)(2,1)}) %all-gather.5.cloned.1.call-update) | async-done | bytes 1048592 | tf_op jit(solution)/shard_map/all_gather | solution.py:14
  48.9 1.6 fusion.36
  50.5 36.8 %all-gather.7.cloned.1.call-done = bf16[1,64,8192]{2,1,0:T(8,128)(2,1)} async-done(((bf16[1,64,512]{2,1,0:T(8,128)(2,1)}), bf16[1,64,8192]{2,1,0:T(8,128)(2,1)}) %all-gather.7.cloned.1.call-update) | async-done | bytes 1048592 | tf_op jit(solution)/shard_map/all_gather | solution.py:14
  87.3 1.5 fusion.40
  88.9 0.0 copy-done
  88.9 0.0 copy-start.1
  88.9 6.7 %fusion.22 = f32[64,896]{1,0:T(8,128)S(1)} fusion(bf16[2,8192,896]{2,1,0:T(8,128)(2,1)} %param.7, bf16[1,64,8192]{2,1,0:T(8,128)(2,1)S(1)} %copy-done, f32[8192]{0:T(1024)S(1)} %bitcast.82, f32[64]{0:T(128)S(1)} %add_rsqrt_fusion.3), kind=kOutput, calls=%fused_computation.22 | convolution fusion | flops 941621248 | bytes 15991040 | tf_op jit(solution)/shard_map/dot_general | solution.py:24
  95.6 6.6 %fusion.20 = f32[64,896]{1,0:T(8,128)S(1)} fusion(bf16[2,8192,896]{2,1,0:T(8,128)(2,1)} %param.7, bf16[1,64,8192]{2,1,0:T(8,128)(2,1)S(1)} %copy-done.1, f32[64]{0:T(128)S(1)} %add_rsqrt_fusion.1, f32[8192]{0:T(1024)S(1)} %bitcast.83), kind=kOutput, calls=%fused_computation.20 | convolution fusion | flops 941621248 | bytes 15991040 | tf_op jit(solution)/shard_map/dot_general | solution.py:24
  102.2 16.4 %fusion.14 = f32[64,8192]{1,0:T(8,128)} fusion(bf16[2,896,8192]{2,1,0:T(8,128)(2,1)} %param.9, bf16[2,8192,896]{2,1,0:T(8,128)(2,1)} %param.8, bf16[1,64,8192]{2,1,0:T(8,128)(2,1)S(1)} %copy-done, f32[8192]{0:T(1024)S(1)} %bitcast.84, f32[64]{0:T(128)S(1)} %add_rsqrt_fusion.3, f32[64,896]{1,0:T(8,128)S(1)} %fusion.22), kind=kOutput, calls=%fused_computation.14 | convolution fusion | flops 1881489408 | bytes 32768256 | tf_op jit(solution)/shard_map/dot_general | solution.py:27
  118.6 16.3 %fusion.12 = f32[64,8192]{1,0:T(8,128)} fusion(bf16[2,896,8192]{2,1,0:T(8,128)(2,1)} %param.9, bf16[2,8192,896]{2,1,0:T(8,128)(2,1)} %param.8, bf16[1,64,8192]{2,1,0:T(8,128)(2,1)S(1)} %copy-done.1, f32[64]{0:T(128)S(1)} %add_rsqrt_fusion.1, f32[8192]{0:T(1024)S(1)} %bitcast.85, f32[64,896]{1,0:T(8,128)S(1)} %fusion.20), kind=kOutput, calls=%fused_computation.12 | convolution fusion | flops 1881489408 | bytes 32768256 | tf_op jit(solution)/shard_map/dot_general | solution.py:27
  134.9 0.0 all-reduce.7.cloned.1.call-update
  134.9 0.2 all-reduce.5.cloned.1.call-start
  135.2 110.9 %all-reduce.7.cloned.1.call-done = (f32[64,8192]{1,0:T(8,128)}, f32[64,8192]{1,0:T(8,128)}) async-done(((f32[64,8192]{1,0:T(8,128)}, f32[64,8192]{1,0:T(8,128)}), (f32[64,8192]{1,0:T(8,128)}, f32[64,8192]{1,0:T(8,128)})) %all-reduce.7.cloned.1.call-update) | async-done | bytes 4194320 | tf_op jit(solution)/shard_map/psum | solution.py:28
  246.0 4.2 %multiply_reduce_fusion = (f32[64]{0:T(128)S(1)}, f32[64,8192]{1,0:T(8,128)}, f32[64]{0:T(128)S(1)}, f32[64,8192]{1,0:T(8,128)S(1)}) fusion(f32[64,8192]{1,0:T(8,128)} %get-tuple-element.7, bf16[1,64,8192]{2,1,0:T(8,128)(2,1)S(1)} %copy-done.1, f32[64,8192]{1,0:T(8,128)} %get-tuple-element.8, bf16[1,64,8192]{2,1,0:T(8,128)(2,1)S(1)} %copy-done), kind=kLoop, calls=%fused_computation.51 | loop fusion | flops 6291328 | bytes 10486272 | tf_op jit(solution)/shard_map/reduce_sum | solution.py:22
  250.2 1.3 copy-done.3
  251.6 6.6 %fusion.10 = f32[64,896]{1,0:T(8,128)S(1)} fusion(bf16[2,8192,896]{2,1,0:T(8,128)(2,1)} %param.7, f32[64,8192]{1,0:T(8,128)S(1)} %get-tuple-element.18, f32[8192]{0:T(1024)S(1)} %bitcast.78, f32[64]{0:T(128)S(1)} %add_rsqrt_fusion.2), kind=kOutput, calls=%fused_computation.10 | convolution fusion | flops 941096960 | bytes 17039616 | tf_op jit(solution)/shard_map/dot_general | solution.py:24
  258.2 14.6 %fusion.2 = f32[64,8192]{1,0:T(8,128)} fusion(bf16[2,896,8192]{2,1,0:T(8,128)(2,1)} %param.9, bf16[2,8192,896]{2,1,0:T(8,128)(2,1)} %param.8, f32[64,896]{1,0:T(8,128)S(1)} %fusion.10, f32[64,8192]{1,0:T(8,128)} %copy-done.3, f32[8192]{0:T(1024)S(1)} %bitcast.79, f32[64]{0:T(128)S(1)} %add_rsqrt_fusion.2), kind=kOutput, calls=%fused_computation.2 | convolution fusion | flops 1880965120 | bytes 33816832 | tf_op jit(solution)/shard_map/dot_general | solution.py:27
  272.8 0.0 copy-done.2
  272.8 6.6 %fusion.8 = f32[64,896]{1,0:T(8,128)S(1)} fusion(bf16[2,8192,896]{2,1,0:T(8,128)(2,1)} %param.7, f32[64,8192]{1,0:T(8,128)S(1)} %copy-done.2, f32[64]{0:T(128)S(1)} %add_rsqrt_fusion, f32[8192]{0:T(1024)S(1)} %bitcast.80), kind=kOutput, calls=%fused_computation.8 | convolution fusion | flops 941096960 | bytes 17039616 | tf_op jit(solution)/shard_map/dot_general | solution.py:24
  279.5 16.4 %fusion = f32[64,8192]{1,0:T(8,128)} fusion(bf16[2,896,8192]{2,1,0:T(8,128)(2,1)} %param.9, bf16[2,8192,896]{2,1,0:T(8,128)(2,1)} %param.8, f32[64,896]{1,0:T(8,128)S(1)} %fusion.8, f32[64,8192]{1,0:T(8,128)S(1)} %copy-done.2, f32[64]{0:T(128)S(1)} %add_rsqrt_fusion, f32[8192]{0:T(1024)S(1)} %bitcast.81), kind=kOutput, calls=%fused_computation | convolution fusion | flops 1880965120 | bytes 33816832 | tf_op jit(solution)/shard_map/dot_general | solution.py:27
  295.8 0.0 all-reduce.5.cloned.1.call-update
  295.9 110.6 %all-reduce.5.cloned.1.call-done = (f32[64,8192]{1,0:T(8,128)}, f32[64,8192]{1,0:T(8,128)}) async-done(((f32[64,8192]{1,0:T(8,128)}, f32[64,8192]{1,0:T(8,128)}), (f32[64,8192]{1,0:T(8,128)}, f32[64,8192]{1,0:T(8,128)})) %all-reduce.5.cloned.1.call-update) | async-done | bytes 4194320 | tf_op jit(solution)/shard_map/psum | solution.py:28
  406.4 1.0 fusion.110
  407.4 0.9 fusion.111
  408.3 0.7 pad_maximum_fusion
  (8 shorter events, 0.0 us)
Async XLA Ops:
  6.5 42.4 %all-gather.5.cloned.1.call-start = ((), (), s32[]{:S(2)}) async-start(), calls=%async_computation | async-start | bytes 1114112 | tf_op jit(solution)/shard_map/all_gather | solution.py:14
  8.1 79.3 %all-gather.7.cloned.1.call-start = ((), (), s32[]{:S(2)}) async-start(), calls=%async_computation.1 | async-start | bytes 1114112 | tf_op jit(solution)/shard_map/all_gather | solution.py:14
  8.8 237.2 %all-reduce.7.cloned.1.call-start = ((), (), s32[]{:S(2)}) async-start(), calls=%async_computation.3 | async-start | bytes 8388608 | tf_op jit(solution)/shard_map/psum | solution.py:28
  48.9 40.0 %copy-start = (bf16[1,64,8192]{2,1,0:T(8,128)(2,1)S(1)}, bf16[1,64,8192]{2,1,0:T(8,128)(2,1)}, u32[]{:S(2)}) copy-start(bf16[1,64,8192]{2,1,0:T(8,128)(2,1)} %all-gather.5.cloned.1.call-done) | copy-start | bytes 3145732
  88.9 6.7 %copy-start.1 = (bf16[1,64,8192]{2,1,0:T(8,128)(2,1)S(1)}, bf16[1,64,8192]{2,1,0:T(8,128)(2,1)}, u32[]{:S(2)}) copy-start(bf16[1,64,8192]{2,1,0:T(8,128)(2,1)} %all-gather.7.cloned.1.call-done) | copy-start | bytes 3145732
  134.9 271.5 %all-reduce.5.cloned.1.call-start = ((), (), s32[]{:S(2)}) async-start(), calls=%async_computation.2 | async-start | bytes 8388608 | tf_op jit(solution)/shard_map/psum | solution.py:28
  250.2 1.4 copy-start.3
  258.2 14.6 %copy-start.2 = (f32[64,8192]{1,0:T(8,128)S(1)}, f32[64,8192]{1,0:T(8,128)}, u32[]{:S(2)}) copy-start(f32[64,8192]{1,0:T(8,128)} %get-tuple-element.12) | copy-start | bytes 6291460
Sparse Core Ops, SparseCore 0:
  9.5 39.3 all-gather.4
  51.0 36.2 all-gather.6
  135.1 110.9 all-reduce.6
  296.0 110.3 all-reduce.4
where the time goes:
time: 416 us
  waiting for transfers between devices  298 us (72%)
  matrix products  90.2 us (22%)
  between operations  13.2 us (3%)
  other arithmetic  9.94 us (2%)
    psum x2, waiting for transfers between devices, body(): branch = lax.psum(partials, 'width')  221 us
    all_gather x2, waiting for transfers between devices, body(): lax.all_gather(stream_in[micro_index], 'width', axis=1, tiled=True)  75.8 us
    dot_general x4, matrix products, body(): jnp.dot(hidden, w_down[depth], preferred_element_type=jnp.float32)  63.7 us
    dot_general x4, matrix products, body(): jnp.dot(normed, w_gate[depth], preferred_element_type=jnp.float32)  26.5 us
  transfers between devices with their start and end apart: 4, of which 4 were waited for; matrix products, arithmetic and copies ran while one was open for 1% of the time, Pallas kernels for 0%

commit v1 on v0

--- a/solution.py
+++ b/solution.py
@@ -2,6 +2,7 @@
 import jax.numpy as jnp
 from jax import lax
 from jax.sharding import PartitionSpec as P
+from jax.lax import all_gather
 
 LAYERS = 2
 MICRO = 2
@@ -25,7 +26,7 @@
             up_out = jnp.dot(normed, w_up[depth], preferred_element_type=jnp.float32)
             hidden = (jax.nn.silu(gate_out) * up_out).astype(jnp.bfloat16)
             partials = jnp.dot(hidden, w_down[depth], preferred_element_type=jnp.float32)
-            branch = lax.psum(partials, "width")
+            branch = all_gather(partials, "width").sum(axis=0)
             stream = (stream_f + branch).astype(jnp.bfloat16)
         results.append(stream)
     results = [lax.dynamic_slice_in_dim(stream, offset, width_local, 1) for stream in results]

time: 416 us -> 788 us (1.89)
  waiting for transfers between devices: 298 us -> 616 us
  other arithmetic: 9.94 us -> 58.7 us
    all_gather x0 -> x4, waiting for transfers between devices: none -> 564 us  [body(): branch = all_gather(partials, 'width').sum(axis=0)]
    psum x2 -> x0, waiting for transfers between devices: 221 us -> none  [body(): branch = lax.psum(partials, 'width')]
    reduce_sum x0 -> x4, other arithmetic: none -> 51.1 us  [body(): branch = all_gather(partials, 'width').sum(axis=0)]
    all_gather x2, waiting for transfers between devices: 75.8 us -> 51.1 us  [body(): lax.all_gather(stream_in[micro_index], 'width', axis=1, tiled=True)]
  transfers between devices with their start and end apart: 4 -> 6, of which waited for: 4 -> 6; matrix products, arithmetic and copies ran while one was open for 1% -> 17% of each run, Pallas kernels for 0% -> 0%
where the time goes in v1:
time: 788 us
  waiting for transfers between devices  616 us (78%)
  matrix products  93.4 us (12%)
  other arithmetic  58.7 us (7%)
  between operations  13.6 us (2%)
    all_gather x4, waiting for transfers between devices, body(): branch = all_gather(partials, 'width').sum(axis=0)  564 us
    dot_general x4, matrix products, body(): jnp.dot(hidden, w_down[depth], preferred_element_type=jnp.float32)  63.1 us
    reduce_sum x4, other arithmetic, body(): branch = all_gather(partials, 'width').sum(axis=0)  51.1 us
    all_gather x2, waiting for transfers between devices, body(): lax.all_gather(stream_in[micro_index], 'width', axis=1, tiled=True)  51.1 us
    dot_general x4, matrix products, body(): jnp.dot(normed, w_gate[depth], preferred_element_type=jnp.float32)  30.3 us
  transfers between devices with their start and end apart: 6, of which 6 were waited for; matrix products, arithmetic and copies ran while one was open for 17% of the time, Pallas kernels for 0%

profile of v1, /device:TPU:0, one launch (start us, length us, event | category | flops | bytes accessed | tf_op | source)
XLA Modules:
  0.0 787.6 jit_solution(9456301840764179438)
XLA Ops:
  6.5 1.5 fusion.118
  8.1 0.7 all-gather.19.cloned.1.call-update
  8.9 1.0 fusion.119
  9.9 39.0 %all-gather.13.cloned.1.call-done = bf16[1,64,8192]{2,1,0:T(8,128)(2,1)} async-done(((bf16[1,64,512]{2,1,0:T(8,128)(2,1)}), bf16[1,64,8192]{2,1,0:T(8,128)(2,1)}) %all-gather.13.cloned.1.call-update) | async-done | bytes 1048592 | tf_op jit(solution)/shard_map/all_gather | solution.py:15
  48.9 1.5 fusion.36
  50.4 8.2 %fusion.22 = f32[64,896]{1,0:T(8,128)S(1)} fusion(bf16[2,8192,896]{2,1,0:T(8,128)(2,1)} %param.7, bf16[1,64,8192]{2,1,0:T(8,128)(2,1)} %all-gather.13.cloned.1.call-done, f32[8192]{0:T(1024)S(1)} %bitcast.90, f32[64]{0:T(128)S(1)} %add_rsqrt_fusion.3), kind=kOutput, calls=%fused_computation.22 | convolution fusion | flops 941621248 | bytes 15991040 | tf_op jit(solution)/shard_map/dot_general | solution.py:25
  58.7 16.3 %fusion.14 = f32[64,8192]{1,0:T(8,128)} fusion(bf16[2,896,8192]{2,1,0:T(8,128)(2,1)} %param.9, bf16[2,8192,896]{2,1,0:T(8,128)(2,1)} %param.8, bf16[1,64,8192]{2,1,0:T(8,128)(2,1)S(1)} %copy-done.1, f32[8192]{0:T(1024)S(1)} %bitcast.91, f32[64]{0:T(128)S(1)} %add_rsqrt_fusion.3, f32[64,896]{1,0:T(8,128)S(1)} %fusion.22), kind=kOutput, calls=%fused_computation.14 | convolution fusion | flops 1881489408 | bytes 32768256 | tf_op jit(solution)/shard_map/dot_general | solution.py:28
  75.0 0.2 all-gather.21.cloned.1.call-start
  75.3 12.1 %all-gather.19.cloned.1.call-done = bf16[1,64,8192]{2,1,0:T(8,128)(2,1)} async-done(((bf16[1,64,512]{2,1,0:T(8,128)(2,1)}), bf16[1,64,8192]{2,1,0:T(8,128)(2,1)}) %all-gather.19.cloned.1.call-update) | async-done | bytes 1048592 | tf_op jit(solution)/shard_map/all_gather | solution.py:15
  87.3 1.5 fusion.40
  88.9 8.2 %fusion.20 = f32[64,896]{1,0:T(8,128)S(1)} fusion(bf16[2,8192,896]{2,1,0:T(8,128)(2,1)} %param.7, bf16[1,64,8192]{2,1,0:T(8,128)(2,1)} %all-gather.19.cloned.1.call-done, f32[64]{0:T(128)S(1)} %add_rsqrt_fusion.1, f32[8192]{0:T(1024)S(1)} %bitcast.92), kind=kOutput, calls=%fused_computation.20 | convolution fusion | flops 941621248 | bytes 15991040 | tf_op jit(solution)/shard_map/dot_general | solution.py:25
  97.1 16.7 %fusion.12 = f32[64,8192]{1,0:T(8,128)} fusion(bf16[2,896,8192]{2,1,0:T(8,128)(2,1)} %param.9, bf16[2,8192,896]{2,1,0:T(8,128)(2,1)} %param.8, bf16[1,64,8192]{2,1,0:T(8,128)(2,1)S(1)} %copy-done, f32[64]{0:T(128)S(1)} %add_rsqrt_fusion.1, f32[8192]{0:T(1024)S(1)} %bitcast.93, f32[64,896]{1,0:T(8,128)S(1)} %fusion.20), kind=kOutput, calls=%fused_computation.12 | convolution fusion | flops 1881489408 | bytes 32768256 | tf_op jit(solution)/shard_map/dot_general | solution.py:28
  113.8 142.8 %all-gather.15.cloned.1.call-done = f32[1024,8192]{1,0:T(8,128)} async-done(((f32[64,8192]{1,0:T(8,128)}), f32[1024,8192]{1,0:T(8,128)}) %all-gather.15.cloned.1.call-update) | async-done | bytes 33554448 | tf_op jit(solution)/shard_map/all_gather | solution.py:29
  256.6 12.7 %reduce_sum.73 = f32[64,8192]{1,0:T(8,128)S(1)} reduce(f32[16,64,8192]{2,1,0:T(8,128)} %bitcast.84, f32[]{:T(128)} %constant.18.clone.1), dimensions={0}, to_apply=%region_1.2 | reduce | flops 7864320 | bytes 35651588 | tf_op jit(solution)/shard_map/reduce_sum | solution.py:29
  269.3 1.6 multiply_reduce_fusion.1
  270.9 1.3 copy-done.2
  272.2 7.0 fusion.10
  279.2 15.0 %fusion.2 = f32[64,8192]{1,0:T(8,128)} fusion(bf16[2,896,8192]{2,1,0:T(8,128)(2,1)} %param.9, bf16[2,8192,896]{2,1,0:T(8,128)(2,1)} %param.8, f32[64,896]{1,0:T(8,128)S(1)} %fusion.10, f32[64,8192]{1,0:T(8,128)} %copy-done.2, f32[8192]{0:T(1024)S(1)} %bitcast.87, f32[64]{0:T(128)S(1)} %add_rsqrt_fusion.2), kind=kOutput, calls=%fused_computation.2 | convolution fusion | flops 1880965120 | bytes 33816832 | tf_op jit(solution)/shard_map/dot_general | solution.py:28
  294.2 0.3 all-gather.23.cloned.1.call-start
  294.5 131.7 %all-gather.21.cloned.1.call-done = f32[1024,8192]{1,0:T(8,128)} async-done(((f32[64,8192]{1,0:T(8,128)}), f32[1024,8192]{1,0:T(8,128)}) %all-gather.21.cloned.1.call-update) | async-done | bytes 33554448 | tf_op jit(solution)/shard_map/all_gather | solution.py:29
  426.1 12.7 %reduce_sum.77 = f32[64,8192]{1,0:T(8,128)S(1)} reduce(f32[16,64,8192]{2,1,0:T(8,128)} %bitcast.83, f32[]{:T(128)} %constant.18.clone.1), dimensions={0}, to_apply=%region_5.6 | reduce | flops 7864320 | bytes 35651588 | tf_op jit(solution)/shard_map/reduce_sum | solution.py:29
  438.8 0.4 multiply_reduce_fusion
  439.2 1.3 copy-done.3
  440.6 6.9 fusion.8
  447.5 15.1 %fusion = f32[64,8192]{1,0:T(8,128)} fusion(bf16[2,896,8192]{2,1,0:T(8,128)(2,1)} %param.9, bf16[2,8192,896]{2,1,0:T(8,128)(2,1)} %param.8, f32[64,896]{1,0:T(8,128)S(1)} %fusion.8, f32[64,8192]{1,0:T(8,128)} %copy-done.3, f32[64]{0:T(128)S(1)} %add_rsqrt_fusion, f32[8192]{0:T(1024)S(1)} %bitcast.89), kind=kOutput, calls=%fused_computation | convolution fusion | flops 1880965120 | bytes 33816832 | tf_op jit(solution)/shard_map/dot_general | solution.py:28
  462.7 132.9 %all-gather.17.cloned.1.call-done = f32[1024,8192]{1,0:T(8,128)} async-done(((f32[64,8192]{1,0:T(8,128)}), f32[1024,8192]{1,0:T(8,128)}) %all-gather.17.cloned.1.call-update) | async-done | bytes 33554448 | tf_op jit(solution)/shard_map/all_gather | solution.py:29
  595.6 12.7 %reduce_sum.75 = f32[64,8192]{1,0:T(8,128)S(1)} reduce(f32[16,64,8192]{2,1,0:T(8,128)} %bitcast.82, f32[]{:T(128)} %constant.18.clone.1), dimensions={0}, to_apply=%region_3.4 | reduce | flops 7864320 | bytes 35651588 | tf_op jit(solution)/shard_map/reduce_sum | solution.py:29
  608.3 156.8 %all-gather.23.cloned.1.call-done = f32[1024,8192]{1,0:T(8,128)} async-done(((f32[64,8192]{1,0:T(8,128)}), f32[1024,8192]{1,0:T(8,128)}) %all-gather.23.cloned.1.call-update) | async-done | bytes 33554448 | tf_op jit(solution)/shard_map/all_gather | solution.py:29
  765.1 13.0 %reduce_sum.79 = f32[64,8192]{1,0:T(8,128)} reduce(f32[16,64,8192]{2,1,0:T(8,128)} %bitcast.85, f32[]{:T(128)} %constant.18.clone.1), dimensions={0}, to_apply=%region_7.8 | reduce | flops 7864320 | bytes 35651588 | tf_op jit(solution)/shard_map/reduce_sum | solution.py:29
  778.1 0.9 fusion.110
  779.1 1.0 fusion.111
  780.1 0.7 pad_maximum_fusion
  (19 shorter events, 0.2 us)
Async XLA Ops:
  6.5 42.4 %all-gather.13.cloned.1.call-start = ((), (), s32[]{:S(2)}) async-start(), calls=%async_computation | async-start | bytes 1114112 | tf_op jit(solution)/shard_map/all_gather | solution.py:15
  8.1 79.2 %all-gather.19.cloned.1.call-start = ((), (), s32[]{:S(2)}) async-start(), calls=%async_computation.3 | async-start | bytes 1114112 | tf_op jit(solution)/shard_map/all_gather | solution.py:15
  8.8 247.8 %all-gather.15.cloned.1.call-start = ((), (), s32[]{:S(2)}) async-start(), calls=%async_computation.1 | async-start | bytes 35651584 | tf_op jit(solution)/shard_map/all_gather | solution.py:29
  50.4 8.2 %copy-start.1 = (bf16[1,64,8192]{2,1,0:T(8,128)(2,1)S(1)}, bf16[1,64,8192]{2,1,0:T(8,128)(2,1)}, u32[]{:S(2)}) copy-start(bf16[1,64,8192]{2,1,0:T(8,128)(2,1)} %all-gather.13.cloned.1.call-done) | copy-start | bytes 3145732
  75.0 351.1 %all-gather.21.cloned.1.call-start = ((), (), s32[]{:S(2)}) async-start(), calls=%async_computation.4 | async-start | bytes 35651584 | tf_op jit(solution)/shard_map/all_gather | solution.py:29
  88.9 8.2 %copy-start = (bf16[1,64,8192]{2,1,0:T(8,128)(2,1)S(1)}, bf16[1,64,8192]{2,1,0:T(8,128)(2,1)}, u32[]{:S(2)}) copy-start(bf16[1,64,8192]{2,1,0:T(8,128)(2,1)} %all-gather.19.cloned.1.call-done) | copy-start | bytes 3145732
  113.8 481.8 %all-gather.17.cloned.1.call-start = ((), (), s32[]{:S(2)}) async-start(), calls=%async_computation.2 | async-start | bytes 35651584 | tf_op jit(solution)/shard_map/all_gather | solution.py:29
  270.9 1.3 copy-start.2
  294.2 470.9 %all-gather.23.cloned.1.call-start = ((), (), s32[]{:S(2)}) async-start(), calls=%async_computation.5 | async-start | bytes 35651584 | tf_op jit(solution)/shard_map/all_gather | solution.py:29
  439.2 1.4 copy-start.3
Sparse Core Ops, SparseCore 0:
  9.5 39.3 all-gather.12
  51.0 36.2 all-gather.18
  88.9 167.6 all-gather.14
  258.1 168.0 all-gather.20
  427.6 168.0 all-gather.16
  597.1 168.0 all-gather.22
